TPU v7x, 128 devices: a whole 4x4x4 slice. The times are simulated.
128 devices in a mesh: rows: 64 (over z, y_hi, x, core), layer: 2 (over y_lo).
Axes of the slice: x: 4, y: 4 (y_hi: 2, y_lo: 2; y = y_hi * 2 + y_lo), z: 4, core: 2. Of those that a mesh axis runs over, the one named last changes fastest.
Arguments:
- gradients: float32 [4096, 32, 2880], P(('layer', 'rows')), parts along dimension 0, may hold values from -6 to 6
- in_basis: bfloat16 [5760, 2880], P(('layer', 'rows')), parts along dimension 0, may hold values from -0.109375 to 0.109375
- out_basis: bfloat16 [4096, 2048], P(('layer', 'rows')), parts along dimension 0, may hold values from -0.125 to 0.125
- eigen_seeds: int32 [5760, 2048], P(('layer', 'rows')), parts along dimension 0, may hold values from 0 to 63
Outputs:
- precond: float32 [4096, 92160], P('layer', 'rows'), parts along dimension 0
There are 2 independent parts, one for each index of `layer`. A program takes and returns all parts, laid end to end along the dimension named above; each array names one. Nothing has to cross between parts.
All inputs are finite; a program needn't handle non-finite values.
Results may differ from a plain program's by a relative error of at most 0.0041.
Values may be sent and summed in bfloat16 or wider, within the bound.
A program may use at most 192 MiB of HBM per device.

v0:
```python
import jax
import jax.numpy as jnp
from jax import lax
from jax.sharding import PartitionSpec as P


def local(gradients, in_basis, out_basis, eigen_seeds):
    devices = lax.axis_size("rows")
    local_rows = gradients.shape[0]
    grads = gradients.shape[1]
    width_in = gradients.shape[2]
    span = width_in // devices
    grad_low = gradients.astype(jnp.bfloat16).reshape(local_rows * grads, width_in)
    full_in = lax.all_gather(in_basis, "rows", axis=0, tiled=True)
    rotated = jnp.dot(grad_low, full_in, preferred_element_type=jnp.float32)
    rotated = rotated.astype(jnp.bfloat16).reshape(local_rows, grads, devices, span)
    rotated = rotated.transpose(0, 2, 3, 1).reshape(local_rows, devices, span * grads)
    moved = lax.all_to_all(rotated, "rows", split_axis=1, concat_axis=0, tiled=True)
    width_out = moved.shape[0]
    moved = moved.reshape(width_out, span * grads)
    full_out = lax.all_gather(out_basis, "rows", axis=0, tiled=True)
    both = lax.dot_general(
        full_out, moved, (((0,), (0,)), ((), ())), preferred_element_type=jnp.float32
    )
    eigval = jnp.exp2(eigen_seeds.astype(jnp.float32) * 0.125 - 4.0)
    denom = (eigval + 0.1).T
    result = both.reshape(width_out, span, grads) / denom[:, :, None]
    return result.reshape(width_out, span * grads)


def solution(mesh):
    placed = (
        P(("layer", "rows"), None, None),
        P(("layer", "rows"), None),
        P(("layer", "rows"), None),
        P(("layer", "rows"), None),
    )
    return jax.shard_map(
        local, mesh=mesh, in_specs=placed, out_specs=P("layer", "rows"), check_vma=False
    )
```

profile of v0, /device:TPU:1, one launch (start us, length us, event | category | flops | bytes accessed | tf_op | source)
XLA Modules:
  0.0 371.2 jit_solution(2633259567758726040)
XLA Ops:
  6.5 0.0 all-gather.6.cloned.1.call-start
  6.5 0.7 all-gather.6.cloned.1.call-update
  7.3 0.0 all-gather.4.cloned.1.call-start
  7.3 0.7 all-gather.4.cloned.1.call-update
  8.0 7.7 %convert_element_type.9 = bf16[32,32,2880]{2,1,0:T(8,128)(2,1)} convert(f32[32,32,2880]{2,1,0:T(8,128)} %param.4) | non-fusion elementwise | flops 2949120 | bytes 17694720 | tf_op jit(solution)/shard_map/convert_element_type | solution.py:13
  15.7 108.6 %all-gather.6.cloned.1.call-done = bf16[64,45,2880]{2,1,0:T(8,128)(2,1)} async-done(((bf16[1,45,2880]{2,1,0:T(8,128)(2,1)}), bf16[64,45,2880]{2,1,0:T(8,128)(2,1)}) %all-gather.6.cloned.1.call-update) | async-done | bytes 16588816 | tf_op jit(solution)/shard_map/all_gather | solution.py:14
  124.3 17.7 %reshape.22 = bf16[2880,2880]{1,0:T(8,128)(2,1)} reshape(bf16[64,45,2880]{2,1,0:T(8,128)(2,1)} %all-gather.6.cloned.1.call-done) | data formatting | bytes 33177600
  142.0 25.6 %convolution_convert_fusion = bf16[1024,2880]{0,1:T(8,128)(2,1)} fusion(bf16[1024,2880]{1,0:T(8,128)(2,1)} %bitcast.21, bf16[2880,2880]{1,0:T(8,128)(2,1)} %reshape.22), kind=kOutput, calls=%fused_computation.1 | convolution fusion | flops 16989880320 | bytes 28385280 | tf_op jit(solution)/shard_map/dot_general | solution.py:15
  167.6 8.5 %copy.8 = bf16[1024,2880]{1,0:T(8,128)(2,1)} copy(bf16[1024,2880]{0,1:T(8,128)(2,1)} %convolution_convert_fusion) | data formatting | bytes 11796480 | tf_op jit(solution)/shard_map/convert_element_type | solution.py:16
  176.1 49.9 %reshape.18 = bf16[32,32,64,45]{3,2,1,0:T(8,128)(2,1)} reshape(bf16[1024,2880]{1,0:T(8,128)(2,1)} %copy.8) | data formatting | bytes 11796480 | tf_op jit(solution)/shard_map/reshape | solution.py:16
  226.0 20.1 %copy.9 = bf16[32,64,45,32]{1,3,2,0:T(8,128)(2,1)} copy(bf16[32,64,45,32]{2,1,3,0:T(8,128)(2,1)} %bitcast.19) | data formatting | bytes 11796480 | tf_op jit(solution)/shard_map/transpose | solution.py:17
  246.1 14.3 %copy.10 = bf16[32,64,1440]{2,0,1:T(8,128)(2,1)} copy(bf16[32,64,1440]{1,2,0:T(8,128)(2,1)} %bitcast.20) | data formatting | bytes 11796480 | tf_op jit(solution)/shard_map/reshape | solution.py:17
  260.5 0.0 copy-start
  260.5 6.2 %all-to-all-start = ((bf16[32,64,1440]{2,0,1:T(8,128)(2,1)}), bf16[32,64,1440]{2,0,1:T(8,128)(2,1)}, u32[]{:S(2)}, u32[]{:S(2)}) async-start(bf16[32,64,1440]{2,0,1:T(8,128)(2,1)} %copy.10), calls=%async_computation | async-start | bytes 12582912 | tf_op jit(solution)/shard_map/all_to_all | solution.py:18
  266.7 0.0 copy-done
  266.7 0.1 add_bitcast_fusion
  266.8 0.0 all-gather.4.cloned.1.call-done
  266.8 78.2 %all-to-all-done = bf16[32,64,1440]{2,0,1:T(8,128)(2,1)} async-done(((bf16[32,64,1440]{2,0,1:T(8,128)(2,1)}), bf16[32,64,1440]{2,0,1:T(8,128)(2,1)}, u32[]{:S(2)}, u32[]{:S(2)}) %all-to-all-start) | async-done | bytes 5898272 | tf_op jit(solution)/shard_map/all_to_all | solution.py:18
  345.0 19.3 %bitcast_divide_fusion = f32[2048,1440]{0,1:T(8,128)} fusion(bf16[2048,1440]{1,0:T(8,128)(2,1)} %bitcast.6, bf16[2048,2048]{1,0:T(8,128)(2,1)} %all-gather.4.cloned.1.call-done, f32[2048,45]{0,1:T(8,128)S(1)} %add_bitcast_fusion), kind=kOutput, calls=%fused_computation | convolution fusion | flops 12082544640 | bytes 26451968 | tf_op jit(solution)/shard_map/dot_general | solution.py:22
Async XLA Ops:
  6.5 117.7 %all-gather.6.cloned.1.call-start = ((), (), s32[]{:S(2)}) async-start(), calls=%async_computation.2 | async-start | bytes 18370560 | tf_op jit(solution)/shard_map/all_gather | solution.py:14
  7.3 259.6 %all-gather.4.cloned.1.call-start = ((), (), s32[]{:S(2)}) async-start(), calls=%async_computation.1 | async-start | bytes 8519680 | tf_op jit(solution)/shard_map/all_gather | solution.py:21
  260.5 6.2 %copy-start = (s32[45,2048]{1,0:T(8,128)S(1)}, s32[45,2048]{1,0:T(8,128)}, u32[]{:S(2)}) copy-start(s32[45,2048]{1,0:T(8,128)} %param.7) | copy-start | bytes 1105924
  260.5 84.6 %all-to-all-start = ((bf16[32,64,1440]{2,0,1:T(8,128)(2,1)}), bf16[32,64,1440]{2,0,1:T(8,128)(2,1)}, u32[]{:S(2)}, u32[]{:S(2)}) async-start(bf16[32,64,1440]{2,0,1:T(8,128)(2,1)} %copy.10), calls=%async_computation | async-start | bytes 12582912 | tf_op jit(solution)/shard_map/all_to_all | solution.py:18
Sparse Core Ops, SparseCore 0:
  10.6 113.5 all-gather.5
  127.6 79.3 all-gather.3
where the time goes:
time: 373 us; the launch traced here: 371 us
  waiting for transfers between devices  188 us (50%)
  local copies, waits for them, and re-layouts  111 us (30%)
  matrix products  44.9 us (12%)
  between operations  13.4 us (4%)
  other arithmetic  7.8 us (2%)
  starting transfers between devices  6.26 us (2%)
    all_gather x1, waiting for transfers between devices, local(): full_in = lax.all_gather(in_basis, 'rows', axis=0, tiled=True)  109 us
    all_to_all x1, waiting for transfers between devices, local(): lax.all_to_all(rotated, 'rows', split_axis=1, concat_axis=0, tiled=True)  78.2 us
    reshape x1, local copies, waits for them, and re-layouts, local(): rotated.astype(jnp.bfloat16).reshape(local_rows, grads, devices, span)  49.9 us
    dot_general x1, matrix products, local(): rotated = jnp.dot(grad_low, full_in, preferred_element_type=jnp.float32)  25.6 us
    transpose x1, local copies, waits for them, and re-layouts, local(): rotated.transpose(0, 2, 3, 1).reshape(local_rows, devices, span * grads)  20.1 us
    dot_general x1, matrix products, local(): lax.dot_general(full_out, moved, (((0,), (0,)), ((), ())), preferred_elem...  19.3 us
    unnamed x3, local copies, waits for them, and re-layouts  17.7 us
    reshape x1, local copies, waits for them, and re-layouts, local(): rotated.transpose(0, 2, 3, 1).reshape(local_rows, devices, span * grads)  14.3 us
  transfers between devices with their start and end apart: 3, of which 2 were waited for; matrix products, arithmetic and copies ran while one was open for 39% of the time, Pallas kernels for 0%

commit v1 on v0

v1 whole, which is shorter than its diff:
```python
import functools

import jax
import jax.numpy as jnp
from jax import lax
from jax.experimental import pallas as pl
from jax.experimental.pallas import tpu as pltpu
from jax.sharding import PartitionSpec as P

LANE = 128
F32 = jnp.float32
BF16 = jnp.bfloat16


def up(value, step):
    return -(-value // step) * step


def windows(span, pad, width):
    found = []
    for tile in range(width // span * pad // LANE):
        real = [
            at // pad * span + at % pad
            for at in range(tile * LANE, tile * LANE + LANE)
            if at % pad < span
        ]
        low = real[0] // LANE * LANE
        found.append((low, min(up(real[-1] + 1, LANE), width)))
    return found


def selector(low, high, tile, span, pad):
    source = low + lax.broadcasted_iota(jnp.int32, (high - low, LANE), 0)
    target = tile * LANE + lax.broadcasted_iota(jnp.int32, (high - low, LANE), 1)
    scale = (1 << 21) // pad + 1
    owner = lax.shift_right_logical(target * scale, 21)
    rest = target - owner * pad
    hit = (source == owner * span + rest) & (rest < span)
    return hit.astype(F32).astype(BF16)


def spread(take, put, span, pad, width):
    for tile, (low, high) in enumerate(windows(span, pad, width)):
        chosen = selector(low, high, tile, span, pad)
        moved = jnp.dot(take(low, high), chosen, preferred_element_type=F32)
        put(tile, moved.astype(BF16))


def pad_kernel(span, pad, width, shard_ref, out_ref):
    out_ref[...] = jnp.zeros_like(out_ref)

    def put(tile, value):
        out_ref[0:span, tile * LANE : (tile + 1) * LANE] = value

    spread(lambda low, high: shard_ref[:, low:high], put, span, pad, width)


def pad_shard(shard, pad):
    span, width = shard.shape
    wide = width // span * pad
    return pl.pallas_call(
        functools.partial(pad_kernel, span, pad, width),
        out_shape=jax.ShapeDtypeStruct((pad, wide), BF16),
        in_specs=[pl.BlockSpec(memory_space=pltpu.VMEM)],
        out_specs=pl.BlockSpec(memory_space=pltpu.VMEM),
    )(shard)


def rotate_kernel(rows, grads, span, pad, width, grad_ref, basis_ref, out_ref, raw, column, low_ref, wide_ref, sem):
    @pl.when(pl.program_id(0) == 0)
    def _():
        copy = pltpu.make_async_copy(grad_ref, raw, sem)
        copy.start()
        copy.wait()
        for left in range(0, width, LANE):
            span_now = min(LANE, width - left)
            column[:, 0:span_now] = raw[:, left : left + span_now]
            for g in range(grads):
                picked = column[pl.ds(g, rows, stride=grads), :].astype(BF16)
                low_ref[g * rows : (g + 1) * rows, left : left + span_now] = picked[:, 0:span_now]

        def put(tile, value):
            wide_ref[:, tile * LANE : (tile + 1) * LANE] = value

        spread(lambda low, high: low_ref[:, low:high], put, span, pad, width)

    turned = jnp.dot(wide_ref[...], basis_ref[...], preferred_element_type=F32)
    out_ref[...] = turned.astype(BF16).T


def rotate(gradients, basis, span, pad):
    rows, grads, width = gradients.shape
    wide = basis.shape[1]
    tile = 256
    return pl.pallas_call(
        functools.partial(rotate_kernel, rows, grads, span, pad, width),
        grid=(wide // tile,),
        out_shape=jax.ShapeDtypeStruct((wide, rows * grads), BF16),
        in_specs=[
            pl.BlockSpec(memory_space=pl.ANY),
            pl.BlockSpec((wide, tile), lambda n: (0, n)),
        ],
        out_specs=pl.BlockSpec((tile, rows * grads), lambda n: (n, 0)),
        scratch_shapes=[
            pltpu.VMEM((rows * grads, width), F32),
            pltpu.VMEM((rows * grads, LANE), F32),
            pltpu.VMEM((rows * grads, width), BF16),
            pltpu.VMEM((rows * grads, wide), BF16),
            pltpu.SemaphoreType.DMA,
        ],
        compiler_params=pltpu.CompilerParams(vmem_limit_bytes=56 << 20),
    )(gradients.reshape(rows * grads, width), basis)


def finish_kernel(grads, span, pad, group, moved_ref, basis_ref, seed_ref, out_ref, eigen_ref, turned_ref):
    rows = LANE // group
    sources = moved_ref.shape[0]

    @pl.when(pl.program_id(0) == 0)
    def _():
        side = group * LANE
        source = lax.broadcasted_iota(jnp.int32, (side, side), 0)
        target = lax.broadcasted_iota(jnp.int32, (side, side), 1)
        inner = source & (rows - 1)
        chunk = lax.shift_right_logical(source & (LANE - 1), rows.bit_length() - 1)
        outer = lax.shift_right_logical(source, LANE.bit_length() - 1)
        swap = (target == chunk * LANE + outer * rows + inner).astype(F32).astype(BF16)
        tiles = grads // group

        def gather(block, carry):
            parts = []
            for tile in range(tiles):
                parts.append(
                    jnp.concatenate(
                        [
                            moved_ref[block * group + s, :, tile * LANE : (tile + 1) * LANE]
                            for s in range(group)
                        ],
                        axis=1,
                    )
                )
            swapped = jnp.dot(jnp.concatenate(parts, axis=0), swap, preferred_element_type=F32).astype(BF16)
            at = pl.ds(pl.multiple_of(block * LANE, LANE), LANE)
            for tile in range(tiles):
                for c in range(group):
                    g = tile * group + c
                    eigen_ref[g * pad : (g + 1) * pad, at] = swapped[
                        tile * pad : (tile + 1) * pad, c * LANE : (c + 1) * LANE
                    ]
            return carry

        lax.fori_loop(0, sources // group, gather, 0)
        turned_ref[...] = jnp.zeros_like(turned_ref)

    both = jnp.dot(eigen_ref[...], basis_ref[...], preferred_element_type=F32)
    value = jnp.exp2(seed_ref[...].astype(F32) * 0.125 - 4.0)
    denom = value + 0.1
    for g in range(grads):
        turned_ref[pl.ds(g, span, stride=grads), :] = both[g * pad : g * pad + span, :] / denom
    out_ref[...] = turned_ref[...].T[:, : span * grads]


def finish(moved, basis, seeds, grads):
    span, pad = seeds.shape[0], moved.shape[1]
    width = basis.shape[0]
    rows = width // moved.shape[0]
    tile = 128
    return pl.pallas_call(
        functools.partial(finish_kernel, grads, span, pad, LANE // rows),
        grid=(width // tile,),
        out_shape=jax.ShapeDtypeStruct((width, span * grads), F32),
        in_specs=[
            pl.BlockSpec(memory_space=pltpu.VMEM),
            pl.BlockSpec((width, tile), lambda n: (0, n)),
            pl.BlockSpec((span, tile), lambda n: (0, n)),
        ],
        out_specs=pl.BlockSpec((tile, span * grads), lambda n: (n, 0)),
        scratch_shapes=[
            pltpu.VMEM((pad * grads, width), BF16),
            pltpu.VMEM((up(span * grads, LANE), tile), F32),
        ],
        compiler_params=pltpu.CompilerParams(vmem_limit_bytes=56 << 20),
    )(moved, basis, seeds)


def local(gradients, in_basis, out_basis, eigen_seeds):
    devices = lax.axis_size("rows")
    rows, grads, width = gradients.shape
    span = in_basis.shape[0]
    pad = up(span, 16)
    shard = pad_shard(in_basis, pad)
    full_in = lax.all_gather(shard, "rows", axis=0, tiled=True)
    full_out = lax.all_gather(out_basis, "rows", axis=0, tiled=True)
    rotated = rotate(gradients, full_in, span, pad)
    rotated = rotated.reshape(devices, pad, rows * grads)
    moved = lax.all_to_all(rotated, "rows", split_axis=0, concat_axis=0, tiled=True)
    return finish(moved, full_out, eigen_seeds, grads)


def solution(mesh):
    placed = (
        P(("layer", "rows"), None, None),
        P(("layer", "rows"), None),
        P(("layer", "rows"), None),
        P(("layer", "rows"), None),
    )
    return jax.shard_map(
        local, mesh=mesh, in_specs=placed, out_specs=P("layer", "rows"), check_vma=False
    )
```

time: 373 us -> 341 us (0.914)
  local copies, waits for them, and re-layouts: 111 us -> 12.2 us
  Pallas kernels: 0 us -> 92.5 us
  matrix products: 44.9 us -> 0 us
  waiting for transfers between devices: 188 us -> 215 us
  other arithmetic: 7.8 us -> 0 us
    all_gather x1, waiting for transfers between devices: 0.02 us -> 97.4 us  [local(): full_out = lax.all_gather(out_basis, 'rows', axis=0, tiled=True)]
    pallas_call x0 -> x3, Pallas kernels: none -> 92.5 us  [the longest x1 50.1 us: finish(): pl.pallas_call(functools.partial(finish_kernel, grads, span, pad, LANE //...]
    all_to_all x1, waiting for transfers between devices: 78.2 us -> 0.01 us  [local(): lax.all_to_all(rotated, 'rows', split_axis=0, concat_axis=0, tiled=True)]
    reshape x2 -> x0, local copies, waits for them, and re-layouts: 64.3 us -> none  [the longest x1 49.9 us: local(): rotated.astype(jnp.bfloat16).reshape(local_rows, grads, devices, span)]
    dot_general x2 -> x0, matrix products: 44.9 us -> none  [the longest x1 25.6 us: local(): rotated = jnp.dot(grad_low, full_in, preferred_element_type=jnp.float32)]
    transpose x1 -> x0, local copies, waits for them, and re-layouts: 20.1 us -> none  [local(): rotated.transpose(0, 2, 3, 1).reshape(local_rows, devices, span * grads)]
    unnamed x3 -> x0, local copies, waits for them, and re-layouts: 17.7 us -> none
    pallas_call x0 -> x1, local copies, waits for them, and re-layouts: none -> 12.2 us  [finish(): pl.pallas_call(functools.partial(finish_kernel, grads, span, pad, LANE //...]
  transfers between devices with their start and end apart: 3 -> 3, of which waited for: 2 -> 2; matrix products, arithmetic and copies ran while one was open for 39% -> 0% of each run, Pallas kernels for 0% -> 12%
where the time goes in v1:
time: 341 us; the launch traced here: 340 us
  waiting for transfers between devices  215 us (63%)
  Pallas kernels  92.5 us (27%)
  between operations  13.4 us (4%)
  local copies, waits for them, and re-layouts  12.2 us (4%)
  starting transfers between devices  6.27 us (2%)
    all_gather x1, waiting for transfers between devices, local(): full_in = lax.all_gather(shard, 'rows', axis=0, tiled=True)  117 us
    all_gather x1, waiting for transfers between devices, local(): full_out = lax.all_gather(out_basis, 'rows', axis=0, tiled=True)  97.4 us
    pallas_call x1, Pallas kernels, finish(): pl.pallas_call(functools.partial(finish_kernel, grads, span, pad, LANE //...  50.1 us
    pallas_call x1, Pallas kernels, rotate(): pl.pallas_call(functools.partial(rotate_kernel, rows, grads, span, pad, w...  40.2 us
    pallas_call x1, local copies, waits for them, and re-layouts, finish(): pl.pallas_call(functools.partial(finish_kernel, grads, span, pad, LANE //...  12.2 us
  transfers between devices with their start and end apart: 3, of which 2 were waited for; matrix products, arithmetic and copies ran while one was open for 0% of the time, Pallas kernels for 12%

profile of v1, /device:TPU:1, one launch (start us, length us, event | category | flops | bytes accessed | tf_op | source)
XLA Modules:
  0.0 339.7 jit_solution(5030609987467294323)
XLA Ops:
  6.5 0.0 all-gather.3.cloned.1.call-start
  6.5 2.2 shard_map.46
  8.7 0.0 all-gather.3.cloned.1.call-update
  8.7 0.0 all-gather.5.cloned.1.call-start
  8.8 0.7 all-gather.5.cloned.1.call-update
  9.5 117.1 %all-gather.3.cloned.1.call-done.basis_ref = bf16[3072,3072]{1,0:T(8,128)(2,1)} async-done(((bf16[48,3072]{1,0:T(8,128)(2,1)}), bf16[3072,3072]{1,0:T(8,128)(2,1)}) %all-gather.3.cloned.1.call-update) | async-done | bytes 18874384 | tf_op jit(solution)/shard_map/all_gather | solution.py:192
  126.6 40.2 %shard_map.47 = bf16[3072,1024]{1,0:T(8,128)(2,1)} custom-call(f32[1024,2880]{1,0:T(8,128)} %bitcast.3, bf16[3072,3072]{1,0:T(8,128)(2,1)} %all-gather.3.cloned.1.call-done.basis_ref), custom_call_target="tpu_custom_call" | custom-call | tf_op jit(solution)/shard_map/pallas_call | solution.py:95
  166.8 6.2 %all-to-all-start = ((bf16[64,48,1024]{2,1,0:T(8,128)(2,1)}), bf16[64,48,1024]{2,1,0:T(8,128)(2,1)}, u32[]{:S(2)}, u32[]{:S(2)}) async-start(bf16[64,48,1024]{2,1,0:T(8,128)(2,1)} %bitcast.2), calls=%async_computation | async-start | bytes 12582912 | tf_op jit(solution)/shard_map/all_to_all | solution.py:196
  173.1 97.4 %all-gather.5.cloned.1.call-done.basis_ref = bf16[2048,2048]{1,0:T(8,128)(2,1)} async-done(((bf16[32,2048]{1,0:T(8,128)(2,1)}), bf16[2048,2048]{1,0:T(8,128)(2,1)}) %all-gather.5.cloned.1.call-update) | async-done | bytes 8388624 | tf_op jit(solution)/shard_map/all_gather | solution.py:193
  270.5 0.0 all-to-all-done.moved_ref
  270.5 50.1 %shard_map.48 = f32[2048,1440]{1,0:T(8,128)} custom-call(bf16[64,48,1024]{2,1,0:T(8,128)(2,1)} %all-to-all-done.moved_ref, bf16[2048,2048]{1,0:T(8,128)(2,1)} %all-gather.5.cloned.1.call-done.basis_ref, s32[45,2048]{1,0:T(8,128)} %seed_ref.1), custom_call_target="tpu_custom_call" | custom-call | tf_op jit(solution)/shard_map/pallas_call | solution.py:168
  320.6 12.2 %copy.5 = f32[2048,1440]{0,1:T(8,128)} copy(f32[2048,1440]{1,0:T(8,128)} %shard_map.48) | data formatting | bytes 23592960 | tf_op jit(solution)/shard_map/pallas_call | solution.py:168
Async XLA Ops:
  6.5 120.1 %all-gather.3.cloned.1.call-start = ((), (), s32[]{:S(2)}) async-start(), calls=%async_computation.1 | async-start | bytes 19169280 | tf_op jit(solution)/shard_map/all_gather | solution.py:192
  8.7 261.8 %all-gather.5.cloned.1.call-start = ((), (), s32[]{:S(2)}) async-start(), calls=%async_computation.2 | async-start | bytes 8519680 | tf_op jit(solution)/shard_map/all_gather | solution.py:193
  166.8 103.7 %all-to-all-start = ((bf16[64,48,1024]{2,1,0:T(8,128)(2,1)}), bf16[64,48,1024]{2,1,0:T(8,128)(2,1)}, u32[]{:S(2)}, u32[]{:S(2)}) async-start(bf16[64,48,1024]{2,1,0:T(8,128)(2,1)} %bitcast.2), calls=%async_computation | async-start | bytes 12582912 | tf_op jit(solution)/shard_map/all_to_all | solution.py:196
Sparse Core Ops, SparseCore 0:
  10.6 115.9 all-gather.2
  129.9 140.5 all-gather.4

commit v2 on v0

v2 whole, which is shorter than its diff:
```python
import functools

import jax
import jax.numpy as jnp
import numpy as np
from jax import lax
from jax.experimental import pallas as pl
from jax.experimental.pallas import tpu as pltpu
from jax.sharding import PartitionSpec as P

LANE = 128
F32 = jnp.float32
BF16 = jnp.bfloat16
MESH = pl.DeviceIdType.MESH
Z, Y, X, CORE = 4, 2, 4, 2
PLANE = Y * X
DEVICES = Z * Y * X * CORE
HOPS = ((0, 0), (0, 1), (0, 3), (1, 0), (0, 2), (1, 1), (1, 3), (1, 2))


def up(value, step):
    return -(-value // step) * step


def device_of(kind, b, y, a):
    z = b * (1 - kind) + a * kind
    x = a * (1 - kind) + b * kind
    return ((z * Y + y) * X + x) * CORE + kind


def slot_of(kind, b, y, a):
    return ((kind * Z + b) * Y + y) * X + a


def wanted(owners, span, pad):
    table = np.full((len(owners), pad), -1, np.int32)
    for place, owner in enumerate(owners):
        table[place, :span] = owner * span + np.arange(span)
    return table.reshape(-1, 1, LANE)


def select(take, table, table_ref, tile):
    picks = table[tile, 0]
    tiles = sorted({int(p) // LANE for p in picks if p >= 0})
    want = jnp.broadcast_to(table_ref[tile], (LANE, LANE))
    row = lax.broadcasted_iota(jnp.int32, (LANE, LANE), 0)
    taken = [take(t) for t in tiles]
    chosen = [
        (want == row + t * LANE).astype(F32).astype(BF16)[: part.shape[1]] for t, part in zip(tiles, taken)
    ]
    moved = jnp.dot(
        jnp.concatenate(taken, axis=1), jnp.concatenate(chosen, axis=0), preferred_element_type=F32
    )
    return moved.astype(BF16)


def rotate_kernel(
    rows, grads, span, pad, width, in_table, col_table,
    shard_ref, low_out_ref, grad_ref, in_table_ref, col_table_ref,
    turned_ref, full_ref,
    units, own, raw, column, low_ref, wide_ref, total, stage,
    w_send, w_recv, o_send, o_recv, raw_sem, own_sem, stage_sem,
):
    me = lax.axis_index("rows")
    kind = me % CORE
    x = (me // CORE) % X
    y = (me // (CORE * X)) % Y
    z = me // (CORE * X * Y)
    a = x * (1 - kind) + z * kind
    b = z * (1 - kind) + x * kind
    other = me + 1 - 2 * kind
    ahead = device_of(kind, (b + 1) % Z, y, a)
    behind = device_of(kind, (b + 3) % Z, y, a)
    wide = pad * DEVICES

    def peer(p):
        dy, da = HOPS[p]
        return (y + dy) % Y, (a + da) % X

    fetch = pltpu.make_async_copy(grad_ref, raw, raw_sem)
    fetch.start()

    barrier = pltpu.get_barrier_semaphore()
    partners = [device_of(kind, b, *peer(p)) for p in range(1, PLANE)] + [ahead, behind, other]
    for partner in partners:
        pl.semaphore_signal(barrier, inc=1, device_id={"rows": partner}, device_id_type=MESH)

    mine = slot_of(kind, b, y, a)
    own[...] = jnp.zeros_like(own)
    for tile in range(wide // LANE):
        own[0:span, tile * LANE : (tile + 1) * LANE] = select(
            lambda t: shard_ref[:, t * LANE : (t + 1) * LANE], col_table, col_table_ref, tile
        )
    pl.semaphore_wait(barrier, len(partners))

    def send_unit(slot, target, source=None):
        pltpu.make_async_remote_copy(
            src_ref=units.at[slot] if source is None else source,
            dst_ref=units.at[slot],
            send_sem=w_send,
            recv_sem=w_recv.at[slot],
            device_id={"rows": target},
            device_id_type=MESH,
        ).start()

    def send_low(owner, target, source=None):
        pltpu.make_async_remote_copy(
            src_ref=full_ref.at[owner] if source is None else source,
            dst_ref=full_ref.at[owner],
            send_sem=o_send,
            recv_sem=o_recv.at[owner],
            device_id={"rows": target},
            device_id_type=MESH,
        ).start()

    def got_unit(slot):
        pltpu.make_async_copy(units.at[slot], units.at[slot], w_recv.at[slot]).wait()

    def got_low(owner):
        pltpu.make_async_copy(full_ref.at[owner], full_ref.at[owner], o_recv.at[owner]).wait()

    class Route:
        def __init__(self, name, send, got):
            self.name, self.send, self.got = name, send, got

        def start(self, source):
            place = self.name(kind, b, y, a)
            for target in [ahead, behind] + partners[: PLANE - 1] + [other]:
                self.send(place, target, source)

        def plane(self, p):
            place = self.name(kind, b, *peer(p))
            self.got(place)
            for target in (ahead, behind, other):
                self.send(place, target)

        def near(self, p):
            place = self.name(kind, (b + 3) % Z, *peer(p))
            self.got(place)
            if p % 2 == 0:
                self.send(place, ahead)
            self.send(place, other)
            place = self.name(kind, (b + 1) % Z, *peer(p))
            self.got(place)
            if p % 2 == 1:
                self.send(place, behind)
            self.send(place, other)

        def far(self, p):
            place = self.name(kind, (b + 2) % Z, *peer(p))
            self.got(place)
            self.send(place, other)

        def beside(self, step):
            for p in range(PLANE):
                dy, da = HOPS[p]
                self.got(self.name(1 - kind, (a + step) % Z, (y + dy) % Y, (b + da) % X))

    basis = Route(slot_of, send_unit, got_unit)
    lows = Route(device_of, send_low, got_low)

    basis.start(own)
    keep = pltpu.make_async_copy(own, units.at[mine], own_sem.at[0])
    keep.start()
    keep_low = pltpu.make_async_copy(low_out_ref, full_ref.at[me], own_sem.at[1])
    keep_low.start()

    fetch.wait()
    count = -(-width // LANE)
    low_ref[:, (count - 1) * LANE :] = jnp.zeros((rows * grads, LANE), BF16)

    def narrow(tile):
        left = tile * LANE
        now = min(LANE, width - left)
        column[:, 0:now] = raw[:, left : left + now]
        for g in range(grads):
            picked = column[pl.ds(g, rows, stride=grads), :].astype(BF16)
            low_ref[g * rows : (g + 1) * rows, left : left + now] = picked[:, 0:now]

    def widen(tile):
        wide_ref[:, tile * LANE : (tile + 1) * LANE] = select(
            lambda t: low_ref[:, t * LANE : (t + 1) * LANE], in_table, in_table_ref, tile
        )

    pieces = [functools.partial(narrow, t) for t in range(count)]
    pieces += [functools.partial(widen, t) for t in range(wide // LANE)]
    events = []
    for p in range(1, PLANE):
        events.append(functools.partial(basis.plane, p))
        events.append(functools.partial(basis.near, p - 1))
    for at, piece in enumerate(pieces):
        piece()
        done = at * len(events) // len(pieces)
        for event in events[done : (at + 1) * len(events) // len(pieces)]:
            event()
    basis.near(PLANE - 1)
    lows.start(low_out_ref)

    block = 256
    blocks = wide // block
    depth = PLANE * pad

    def part(step, n):
        at = pl.ds(pl.multiple_of(n * block, block), block)
        lefts, rights = [], []
        for what, where in ((kind, b), (1 - kind, a)):
            group = what * Z + (where + step) % Z
            lefts.append(wide_ref[:, pl.ds(pl.multiple_of(group * depth, LANE), depth)])
            rights.append(units[pl.ds(group * PLANE, PLANE), :, at].reshape(depth, block))
        return jnp.dot(
            jnp.concatenate(lefts, axis=1), jnp.concatenate(rights, axis=0), preferred_element_type=F32
        )

    def multiply(step, first, last):
        def body(n, carry):
            at = pl.ds(pl.multiple_of(n * block, block), block)
            if step == 0:
                total[:, at] = part(step, n)
            else:
                total[:, at] += part(step, n)
            return carry

        lax.fori_loop(first, last, body, 0)

    keep.wait()
    keep_low.wait()
    third = blocks // 3
    basis.beside(0)
    multiply(0, 0, third)
    lows.plane(1)
    multiply(0, third, 2 * third)
    lows.near(0)
    lows.plane(2)
    multiply(0, 2 * third, blocks)
    lows.near(1)
    lows.plane(3)
    basis.beside(1)
    multiply(1, 0, third)
    lows.near(2)
    lows.plane(4)
    multiply(1, third, 2 * third)
    lows.near(3)
    lows.plane(5)
    multiply(1, 2 * third, blocks)
    lows.near(4)
    lows.plane(6)
    basis.beside(3)
    multiply(3, 0, third)
    lows.near(5)
    lows.plane(7)
    multiply(3, third, 2 * third)
    lows.near(6)
    lows.near(7)
    multiply(3, 2 * third, blocks)
    for p in range(PLANE):
        basis.far(p)
    basis.beside(2)

    def out_copy(n):
        return pltpu.make_async_copy(
            stage.at[n % 2],
            turned_ref.at[pl.ds(pl.multiple_of(n * block, block), block)],
            stage_sem.at[n % 2],
        )

    def last(n, carry):
        at = pl.ds(pl.multiple_of(n * block, block), block)

        @pl.when(n >= 2)
        def _():
            out_copy(n - 2).wait()

        stage[n % 2] = (total[:, at] + part(2, n)).astype(BF16).T
        out_copy(n).start()
        return carry

    lax.fori_loop(0, third, last, 0)
    for p in range(PLANE // 2):
        lows.far(p)
    lax.fori_loop(third, 2 * third, last, 0)
    for p in range(PLANE // 2, PLANE):
        lows.far(p)
    lax.fori_loop(2 * third, blocks, last, 0)
    out_copy(blocks - 2).wait()
    out_copy(blocks - 1).wait()
    for step in range(Z):
        lows.beside(step)
    sends = PLANE + 2 + 3 * (PLANE - 1) + 3 * PLANE + PLANE
    pltpu.make_async_copy(units.at[pl.ds(0, sends)], units.at[pl.ds(0, sends)], w_send).wait()
    pltpu.make_async_copy(full_ref.at[pl.ds(0, sends)], full_ref.at[pl.ds(0, sends)], o_send).wait()


def rotate(gradients, shard, low_out, pad):
    rows, grads, width = gradients.shape
    span = shard.shape[0]
    wide = pad * DEVICES
    in_owners = [
        device_of(kind, b, y, a)
        for kind in range(CORE)
        for b in range(Z)
        for y in range(Y)
        for a in range(X)
    ]
    in_table = wanted(in_owners, span, pad)
    col_table = wanted(list(range(DEVICES)), span, pad)
    any_space = pl.BlockSpec(memory_space=pl.ANY)
    vmem = pl.BlockSpec(memory_space=pltpu.VMEM)
    block = 256
    return pl.pallas_call(
        functools.partial(rotate_kernel, rows, grads, span, pad, width, in_table, col_table),
        out_shape=(
            jax.ShapeDtypeStruct((wide, rows * grads), BF16),
            jax.ShapeDtypeStruct((DEVICES,) + low_out.shape, BF16),
        ),
        in_specs=[vmem, any_space, any_space, vmem, vmem],
        out_specs=(any_space, any_space),
        scratch_shapes=[
            pltpu.VMEM((DEVICES, pad, wide), BF16),
            pltpu.VMEM((pad, wide), BF16),
            pltpu.VMEM((rows * grads, width), F32),
            pltpu.VMEM((rows * grads, LANE), F32),
            pltpu.VMEM((rows * grads, up(width, LANE)), BF16),
            pltpu.VMEM((rows * grads, wide), BF16),
            pltpu.VMEM((rows * grads, wide), F32),
            pltpu.VMEM((2, block, rows * grads), BF16),
            pltpu.SemaphoreType.DMA,
            pltpu.SemaphoreType.DMA((DEVICES,)),
            pltpu.SemaphoreType.DMA,
            pltpu.SemaphoreType.DMA((DEVICES,)),
            pltpu.SemaphoreType.DMA,
            pltpu.SemaphoreType.DMA((2,)),
            pltpu.SemaphoreType.DMA((2,)),
        ],
        compiler_params=pltpu.CompilerParams(
            vmem_limit_bytes=60 << 20, collective_id=0, has_side_effects=True
        ),
    )(
        shard,
        low_out,
        gradients.reshape(rows * grads, width),
        jnp.asarray(in_table),
        jnp.asarray(col_table),
    )


def finish_kernel(grads, span, pad, group, moved_ref, basis_ref, seed_ref, out_ref, eigen_ref, ready, sem):
    rows = LANE // group
    sources = moved_ref.shape[0]
    step = pl.program_id(0)
    tile = basis_ref.shape[1]
    halves = tile // LANE

    @pl.when(step == 0)
    def _():
        side = group * LANE
        source = lax.broadcasted_iota(jnp.int32, (side, side), 0)
        target = lax.broadcasted_iota(jnp.int32, (side, side), 1)
        inner = source & (rows - 1)
        chunk = lax.shift_right_logical(source & (LANE - 1), rows.bit_length() - 1)
        outer = lax.shift_right_logical(source, LANE.bit_length() - 1)
        swap = (target == chunk * LANE + outer * rows + inner).astype(F32).astype(BF16)
        tiles = grads // group

        def gather(block, carry):
            parts = []
            for tile in range(tiles):
                parts.append(
                    jnp.concatenate(
                        [
                            moved_ref[block * group + s, :, tile * LANE : (tile + 1) * LANE]
                            for s in range(group)
                        ],
                        axis=1,
                    )
                )
            swapped = jnp.dot(jnp.concatenate(parts, axis=0), swap, preferred_element_type=F32).astype(BF16)
            at = pl.ds(pl.multiple_of(block * LANE, LANE), LANE)
            for tile in range(tiles):
                for c in range(group):
                    g = tile * group + c
                    eigen_ref[g * pad : (g + 1) * pad, at] = swapped[
                        tile * pad : (tile + 1) * pad, c * LANE : (c + 1) * LANE
                    ]
            return carry

        lax.fori_loop(0, sources // group, gather, 0)

    def out_copy(which, half):
        return pltpu.make_async_copy(
            ready.at[which % 2, half],
            out_ref.at[:, pl.ds(pl.multiple_of((which * halves + half) * LANE, LANE), LANE)],
            sem.at[which % 2, half],
        )

    @pl.when(step >= 2)
    def _():
        for half in range(halves):
            out_copy(step - 2, half).wait()

    value = jnp.exp2(seed_ref[...].astype(F32) * 0.125 - 4.0)
    denom = value + 0.1
    for g in range(0, grads, 8):
        both = jnp.dot(eigen_ref[g * pad : (g + 8) * pad, :], basis_ref[...], preferred_element_type=F32)
        for d in range(8):
            result = both[d * pad : d * pad + span, :] / denom
            for half in range(halves):
                ready[step % 2, half, pl.ds(g + d, span, stride=grads), :] = result[
                    :, half * LANE : (half + 1) * LANE
                ]
    for half in range(halves):
        out_copy(step, half).start()

    @pl.when(step == pl.num_programs(0) - 1)
    def _():
        for half in range(halves):
            out_copy(step - 1, half).wait()
            out_copy(step, half).wait()


def finish(moved, basis, seeds, grads):
    span, pad = seeds.shape[0], moved.shape[1]
    width = basis.shape[0]
    rows = width // moved.shape[0]
    tile = 256
    return pl.pallas_call(
        functools.partial(finish_kernel, grads, span, pad, LANE // rows),
        grid=(width // tile,),
        out_shape=jax.ShapeDtypeStruct((span * grads, width), F32),
        in_specs=[
            pl.BlockSpec(memory_space=pltpu.VMEM),
            pl.BlockSpec((width, tile), lambda n: (0, n)),
            pl.BlockSpec((span, tile), lambda n: (0, n)),
        ],
        out_specs=pl.BlockSpec(memory_space=pl.ANY),
        scratch_shapes=[
            pltpu.VMEM((pad * grads, width), BF16),
            pltpu.VMEM((2, tile // LANE, span * grads, LANE), F32),
            pltpu.SemaphoreType.DMA((2, tile // LANE)),
        ],
        compiler_params=pltpu.CompilerParams(vmem_limit_bytes=56 << 20),
    )(moved, basis, seeds)


def local(gradients, in_basis, out_basis, eigen_seeds):
    rows, grads, width = gradients.shape
    pad = up(in_basis.shape[0], 16)
    rotated, full_out = rotate(gradients, in_basis, out_basis, pad)
    rotated = rotated.reshape(DEVICES, pad, rows * grads)
    moved = lax.all_to_all(rotated, "rows", split_axis=0, concat_axis=0, tiled=True)
    full_out = full_out.reshape(-1, out_basis.shape[1])
    return finish(moved, full_out, eigen_seeds, grads).T


def solution(mesh):
    placed = (
        P(("layer", "rows"), None, None),
        P(("layer", "rows"), None),
        P(("layer", "rows"), None),
        P(("layer", "rows"), None),
    )
    return jax.shard_map(
        local, mesh=mesh, in_specs=placed, out_specs=P("layer", "rows"), check_vma=False
    )
```

time: 373 us -> 226 us (0.61)
  waiting for transfers between devices: 188 us -> 0 us
  Pallas kernels: 0 us -> 141 us
  local copies, waits for them, and re-layouts: 111 us -> 0 us
  blocking collectives: 0 us -> 84.6 us
  matrix products: 44.9 us -> 0 us
  between operations: 13.4 us -> 0.19 us
  other arithmetic: 7.8 us -> 0 us
  starting transfers between devices: 6.26 us -> 0 us
    pallas_call x0 -> x2, Pallas kernels: none -> 141 us  [the longest x1 108 us: rotate(): pl.pallas_call(functools.partial(rotate_kernel, rows, grads, span, pad, w...]
    all_gather x2 -> x0, waiting for transfers between devices: 109 us -> none  [the longest x1 109 us: local(): full_in = lax.all_gather(in_basis, 'rows', axis=0, tiled=True)]
    all_to_all x0 -> x1, blocking collectives: none -> 84.6 us  [local(): lax.all_to_all(rotated, 'rows', split_axis=0, concat_axis=0, tiled=True)]
    all_to_all x1 -> x0, waiting for transfers between devices: 78.2 us -> none  [local(): lax.all_to_all(rotated, 'rows', split_axis=1, concat_axis=0, tiled=True)]
    reshape x2 -> x0, local copies, waits for them, and re-layouts: 64.3 us -> none  [the longest x1 49.9 us: local(): rotated.astype(jnp.bfloat16).reshape(local_rows, grads, devices, span)]
    dot_general x2 -> x0, matrix products: 44.9 us -> none  [the longest x1 25.6 us: local(): rotated = jnp.dot(grad_low, full_in, preferred_element_type=jnp.float32)]
    transpose x1 -> x0, local copies, waits for them, and re-layouts: 20.1 us -> none  [local(): rotated.transpose(0, 2, 3, 1).reshape(local_rows, devices, span * grads)]
    unnamed x3 -> x0, local copies, waits for them, and re-layouts: 17.7 us -> none
  transfers between devices with their start and end apart: 3 -> 0, of which waited for: 2 -> 0; matrix products, arithmetic and copies ran while one was open for 39% -> 0% of each run, Pallas kernels for 0% -> 0%
where the time goes in v2:
time: 226 us
  Pallas kernels  141 us (62%)
  blocking collectives  84.6 us (37%)
    pallas_call x1, Pallas kernels, rotate(): pl.pallas_call(functools.partial(rotate_kernel, rows, grads, span, pad, w...  108 us
    all_to_all x1, blocking collectives, local(): lax.all_to_all(rotated, 'rows', split_axis=0, concat_axis=0, tiled=True)  84.6 us
    pallas_call x1, Pallas kernels, finish(): pl.pallas_call(functools.partial(finish_kernel, grads, span, pad, LANE //...  32.5 us

profile of v2, /device:TPU:1, one launch (start us, length us, event | category | flops | bytes accessed | tf_op | source)
XLA Modules:
  0.0 225.5 jit_solution(16245089207588893681)
XLA Ops:
  0.0 108.3 %shard_map.64 = (bf16[3072,1024]{1,0:T(8,128)(2,1)}, bf16[64,32,2048]{2,1,0:T(8,128)(2,1)}) custom-call(bf16[45,2880]{1,0:T(8,128)(2,1)} %shard_ref.1, bf16[32,2048]{1,0:T(8,128)(2,1)} %low_out_ref.1, f32[1024,2880]{1,0:T(8,128)} %bitcast.4, s32[24,1,128]{2,1,0:T(1,128)} %constant.4.clone.in_table_ref, s32[24,1,128]{2,1,0:T(1,128)} %constant.5.clone.col_table_ref), custom_call_target="tpu_custom_call" | custom-call | tf_op jit(solution)/shard_map/pallas_call | solution.py:309
  108.3 84.6 %all_to_all.5.moved_ref = bf16[64,48,1024]{2,1,0:T(8,128)(2,1)} all-to-all(bf16[64,48,1024]{2,1,0:T(8,128)(2,1)} %bitcast.6), channel_id=1, replica_groups=mesh['rows'=64,'layer'=2] {'rows'}, dimensions={0} | all-to-all | bytes 12582912 | tf_op jit(solution)/shard_map/all_to_all | solution.py:449
  192.8 32.5 %shard_map.65 = f32[1440,2048]{1,0:T(8,128)} custom-call(bf16[64,48,1024]{2,1,0:T(8,128)(2,1)} %all_to_all.5.moved_ref, bf16[2048,2048]{1,0:T(8,128)(2,1)} %bitcast.5, s32[45,2048]{1,0:T(8,128)} %seed_ref.1), custom_call_target="tpu_custom_call" | custom-call | tf_op jit(solution)/shard_map/pallas_call | solution.py:425

commit v3 on v2

--- a/solution.py
+++ b/solution.py
@@ -15,7 +15,7 @@
 Z, Y, X, CORE = 4, 2, 4, 2
 PLANE = Y * X
 DEVICES = Z * Y * X * CORE
-HOPS = ((0, 0), (0, 1), (0, 3), (1, 0), (0, 2), (1, 1), (1, 3), (1, 2))
+HOPS = ((0, 0), (1, 0), (0, 1), (0, 3), (1, 1), (1, 3), (0, 2), (1, 2))
 
 
 def up(value, step):
@@ -81,9 +81,28 @@
     fetch.start()
 
     barrier = pltpu.get_barrier_semaphore()
-    partners = [device_of(kind, b, *peer(p)) for p in range(1, PLANE)] + [ahead, behind, other]
+    across = device_of(kind, b, 1 - y, a)
+    right = device_of(kind, b, y, (a + 1) % X)
+    left = device_of(kind, b, y, (a + 3) % X)
+    partners = [ahead, behind, right, left, across, other]
     for partner in partners:
         pl.semaphore_signal(barrier, inc=1, device_id={"rows": partner}, device_id_type=MESH)
+
+    def send_low(owner, target, source=None):
+        pltpu.make_async_remote_copy(
+            src_ref=full_ref.at[owner] if source is None else source,
+            dst_ref=full_ref.at[owner],
+            send_sem=o_send,
+            recv_sem=o_recv.at[owner],
+            device_id={"rows": target},
+            device_id_type=MESH,
+        ).start()
+
+    pl.semaphore_wait(barrier, len(partners))
+    for target in (right, left, ahead, behind, across, other):
+        send_low(me, target, low_out_ref)
+    keep_low = pltpu.make_async_copy(low_out_ref, full_ref.at[me], own_sem.at[1])
+    keep_low.start()
 
     mine = slot_of(kind, b, y, a)
     own[...] = jnp.zeros_like(own)
@@ -91,7 +110,6 @@
         own[0:span, tile * LANE : (tile + 1) * LANE] = select(
             lambda t: shard_ref[:, t * LANE : (t + 1) * LANE], col_table, col_table_ref, tile
         )
-    pl.semaphore_wait(barrier, len(partners))
 
     def send_unit(slot, target, source=None):
         pltpu.make_async_remote_copy(
@@ -103,67 +121,87 @@
             device_id_type=MESH,
         ).start()
 
-    def send_low(owner, target, source=None):
-        pltpu.make_async_remote_copy(
-            src_ref=full_ref.at[owner] if source is None else source,
-            dst_ref=full_ref.at[owner],
-            send_sem=o_send,
-            recv_sem=o_recv.at[owner],
-            device_id={"rows": target},
-            device_id_type=MESH,
-        ).start()
-
     def got_unit(slot):
         pltpu.make_async_copy(units.at[slot], units.at[slot], w_recv.at[slot]).wait()
 
     def got_low(owner):
         pltpu.make_async_copy(full_ref.at[owner], full_ref.at[owner], o_recv.at[owner]).wait()
 
-    class Route:
-        def __init__(self, name, send, got):
-            self.name, self.send, self.got = name, send, got
-
-        def start(self, source):
-            place = self.name(kind, b, y, a)
-            for target in [ahead, behind] + partners[: PLANE - 1] + [other]:
-                self.send(place, target, source)
-
-        def plane(self, p):
-            place = self.name(kind, b, *peer(p))
-            self.got(place)
-            for target in (ahead, behind, other):
-                self.send(place, target)
-
-        def near(self, p):
-            place = self.name(kind, (b + 3) % Z, *peer(p))
-            self.got(place)
-            if p % 2 == 0:
-                self.send(place, ahead)
-            self.send(place, other)
-            place = self.name(kind, (b + 1) % Z, *peer(p))
-            self.got(place)
-            if p % 2 == 1:
-                self.send(place, behind)
-            self.send(place, other)
-
-        def far(self, p):
-            place = self.name(kind, (b + 2) % Z, *peer(p))
-            self.got(place)
-            self.send(place, other)
-
-        def beside(self, step):
-            for p in range(PLANE):
-                dy, da = HOPS[p]
-                self.got(self.name(1 - kind, (a + step) % Z, (y + dy) % Y, (b + da) % X))
-
-    basis = Route(slot_of, send_unit, got_unit)
-    lows = Route(device_of, send_low, got_low)
-
-    basis.start(own)
+    def plane(p):
+        place = slot_of(kind, b, *peer(p))
+        got_unit(place)
+        hop = HOPS[p]
+        if hop in ((1, 0), (0, 3)):
+            send_unit(place, right)
+        if hop in ((1, 0), (1, 1)):
+            send_unit(place, left)
+        for target in (ahead, behind, other):
+            send_unit(place, target)
+
+    def near(p):
+        place = slot_of(kind, (b + 3) % Z, *peer(p))
+        got_unit(place)
+        if p % 2 == 0:
+            send_unit(place, ahead)
+        send_unit(place, other)
+        place = slot_of(kind, (b + 1) % Z, *peer(p))
+        got_unit(place)
+        if p % 2 == 1:
+            send_unit(place, behind)
+        send_unit(place, other)
+
+    def far(p):
+        place = slot_of(kind, (b + 2) % Z, *peer(p))
+        got_unit(place)
+        send_unit(place, other)
+
+    def beside(step):
+        for dy, da in HOPS:
+            got_unit(slot_of(1 - kind, (a + step) % Z, (y + dy) % Y, (b + da) % X))
+
+    def low_row(da):
+        owner = device_of(kind, b, y, (a + da) % X)
+        got_low(owner)
+        if da == 3:
+            send_low(owner, right)
+        for target in (ahead, behind, across, other):
+            send_low(owner, target)
+
+    def low_near(da):
+        owner = device_of(kind, (b + 3) % Z, y, (a + da) % X)
+        got_low(owner)
+        if da < 2:
+            send_low(owner, ahead)
+        for target in (across, other):
+            send_low(owner, target)
+        owner = device_of(kind, (b + 1) % Z, y, (a + da) % X)
+        got_low(owner)
+        if da >= 2:
+            send_low(owner, behind)
+        for target in (across, other):
+            send_low(owner, target)
+
+    def low_far(da):
+        owner = device_of(kind, (b + 2) % Z, y, (a + da) % X)
+        got_low(owner)
+        for target in (across, other):
+            send_low(owner, target)
+
+    def low_across(db, da):
+        owner = device_of(kind, (b + db) % Z, 1 - y, (a + da) % X)
+        got_low(owner)
+        send_low(owner, other)
+
+    def low_beside():
+        for db in range(Z):
+            for dy in range(Y):
+                for da in range(X):
+                    got_low(device_of(1 - kind, (a + db) % Z, (y + dy) % Y, (b + da) % X))
+
+    for target in (ahead, behind, right, left, across, other):
+        send_unit(mine, target, own)
     keep = pltpu.make_async_copy(own, units.at[mine], own_sem.at[0])
     keep.start()
-    keep_low = pltpu.make_async_copy(low_out_ref, full_ref.at[me], own_sem.at[1])
-    keep_low.start()
 
     fetch.wait()
     count = -(-width // LANE)
@@ -184,17 +222,17 @@
 
     pieces = [functools.partial(narrow, t) for t in range(count)]
     pieces += [functools.partial(widen, t) for t in range(wide // LANE)]
-    events = []
-    for p in range(1, PLANE):
-        events.append(functools.partial(basis.plane, p))
-        events.append(functools.partial(basis.near, p - 1))
+    step = functools.partial
+    events = [
+        step(low_row, 3), step(low_row, 1), step(plane, 1), step(low_near, 0), step(plane, 2), step(plane, 3),
+        step(near, 0), step(low_row, 2), step(low_near, 3), step(plane, 4), step(plane, 5), step(low_near, 1),
+        step(near, 1), step(low_near, 2), step(plane, 6), step(near, 2), step(plane, 7), step(near, 3),
+    ]
     for at, piece in enumerate(pieces):
         piece()
         done = at * len(events) // len(pieces)
         for event in events[done : (at + 1) * len(events) // len(pieces)]:
             event()
-    basis.near(PLANE - 1)
-    lows.start(low_out_ref)
 
     block = 256
     blocks = wide // block
@@ -225,36 +263,41 @@
     keep.wait()
     keep_low.wait()
     third = blocks // 3
-    basis.beside(0)
+    beside(0)
     multiply(0, 0, third)
-    lows.plane(1)
+    low_far(0)
+    low_far(1)
+    near(4)
     multiply(0, third, 2 * third)
-    lows.near(0)
-    lows.plane(2)
+    low_far(2)
+    low_far(3)
+    near(5)
     multiply(0, 2 * third, blocks)
-    lows.near(1)
-    lows.plane(3)
-    basis.beside(1)
+    near(6)
+    near(7)
+    for da in range(X):
+        low_across(0, da)
+    beside(1)
     multiply(1, 0, third)
-    lows.near(2)
-    lows.plane(4)
+    far(0)
     multiply(1, third, 2 * third)
-    lows.near(3)
-    lows.plane(5)
+    far(1)
     multiply(1, 2 * third, blocks)
-    lows.near(4)
-    lows.plane(6)
-    basis.beside(3)
+    far(2)
+    for da in range(X):
+        low_across(3, da)
+    beside(3)
     multiply(3, 0, third)
-    lows.near(5)
-    lows.plane(7)
+    far(3)
     multiply(3, third, 2 * third)
-    lows.near(6)
-    lows.near(7)
+    far(4)
     multiply(3, 2 * third, blocks)
-    for p in range(PLANE):
-        basis.far(p)
-    basis.beside(2)
+    far(5)
+    for da in range(X):
+        low_across(1, da)
+    far(6)
+    far(7)
+    beside(2)
 
     def out_copy(n):
         return pltpu.make_async_copy(
@@ -275,19 +318,16 @@
         return carry
 
     lax.fori_loop(0, third, last, 0)
-    for p in range(PLANE // 2):
-        lows.far(p)
-    lax.fori_loop(third, 2 * third, last, 0)
-    for p in range(PLANE // 2, PLANE):
-        lows.far(p)
-    lax.fori_loop(2 * third, blocks, last, 0)
+    for da in range(X):
+        low_across(2, da)
+    lax.fori_loop(third, blocks, last, 0)
     out_copy(blocks - 2).wait()
     out_copy(blocks - 1).wait()
-    for step in range(Z):
-        lows.beside(step)
-    sends = PLANE + 2 + 3 * (PLANE - 1) + 3 * PLANE + PLANE
+    low_beside()
+    sends = 6 + 4 + 3 * (PLANE - 1) + 3 * PLANE + PLANE
     pltpu.make_async_copy(units.at[pl.ds(0, sends)], units.at[pl.ds(0, sends)], w_send).wait()
-    pltpu.make_async_copy(full_ref.at[pl.ds(0, sends)], full_ref.at[pl.ds(0, sends)], o_send).wait()
+    lows = 6 + 1 + 4 * (X - 1) + 5 * X + 2 * X + Z * X
+    pltpu.make_async_copy(full_ref.at[pl.ds(0, lows)], full_ref.at[pl.ds(0, lows)], o_send).wait()
 
 
 def rotate(gradients, shard, low_out, pad):

time: 226 us -> 208 us (0.920)
  Pallas kernels: 141 us -> 125 us
    pallas_call x1, Pallas kernels: 108 us -> 92.6 us  [rotate(): pl.pallas_call(functools.partial(rotate_kernel, rows, grads, span, pad, w...]
where the time goes in v3:
time: 208 us
  Pallas kernels  125 us (60%)
  blocking collectives  82.8 us (40%)
    pallas_call x1, Pallas kernels, rotate(): pl.pallas_call(functools.partial(rotate_kernel, rows, grads, span, pad, w...  92.6 us
    all_to_all x1, blocking collectives, local(): lax.all_to_all(rotated, 'rows', split_axis=0, concat_axis=0, tiled=True)  82.8 us
    pallas_call x1, Pallas kernels, finish(): pl.pallas_call(functools.partial(finish_kernel, grads, span, pad, LANE //...  32.5 us

profile of v3, /device:TPU:1, one launch (start us, length us, event | category | flops | bytes accessed | tf_op | source)
XLA Modules:
  0.0 208.1 jit_solution(7829063006074885159)
XLA Ops:
  0.0 92.6 %shard_map.64 = (bf16[3072,1024]{1,0:T(8,128)(2,1)}, bf16[64,32,2048]{2,1,0:T(8,128)(2,1)}) custom-call(bf16[45,2880]{1,0:T(8,128)(2,1)} %shard_ref.1, bf16[32,2048]{1,0:T(8,128)(2,1)} %low_out_ref.1, f32[1024,2880]{1,0:T(8,128)} %bitcast.4, s32[24,1,128]{2,1,0:T(1,128)} %constant.4.clone.in_table_ref, s32[24,1,128]{2,1,0:T(1,128)} %constant.5.clone.col_table_ref), custom_call_target="tpu_custom_call" | custom-call | tf_op jit(solution)/shard_map/pallas_call | solution.py:349
  92.7 82.8 %all_to_all.5.moved_ref = bf16[64,48,1024]{2,1,0:T(8,128)(2,1)} all-to-all(bf16[64,48,1024]{2,1,0:T(8,128)(2,1)} %bitcast.6), channel_id=1, replica_groups=mesh['rows'=64,'layer'=2] {'rows'}, dimensions={0} | all-to-all | bytes 12582912 | tf_op jit(solution)/shard_map/all_to_all | solution.py:489
  175.4 32.5 %shard_map.65 = f32[1440,2048]{1,0:T(8,128)} custom-call(bf16[64,48,1024]{2,1,0:T(8,128)(2,1)} %all_to_all.5.moved_ref, bf16[2048,2048]{1,0:T(8,128)(2,1)} %bitcast.5, s32[45,2048]{1,0:T(8,128)} %seed_ref.1), custom_call_target="tpu_custom_call" | custom-call | tf_op jit(solution)/shard_map/pallas_call | solution.py:465

commit v4 on v3

--- a/solution.py
+++ b/solution.py
@@ -58,7 +58,7 @@
     rows, grads, span, pad, width, in_table, col_table,
     shard_ref, low_out_ref, grad_ref, in_table_ref, col_table_ref,
     turned_ref, full_ref,
-    units, own, raw, column, low_ref, wide_ref, total, stage,
+    units, own, raw, column, low_ref, wide_ref, total, spread, stage,
     w_send, w_recv, o_send, o_recv, raw_sem, own_sem, stage_sem,
 ):
     me = lax.axis_index("rows")
@@ -77,8 +77,12 @@
         dy, da = HOPS[p]
         return (y + dy) % Y, (a + da) % X
 
-    fetch = pltpu.make_async_copy(grad_ref, raw, raw_sem)
-    fetch.start()
+    part_rows = raw.shape[0] // grads
+
+    def fetch(part):
+        return pltpu.make_async_copy(grad_ref.at[pl.ds(part * raw.shape[0], raw.shape[0])], raw, raw_sem)
+
+    fetch(0).start()
 
     barrier = pltpu.get_barrier_semaphore()
     across = device_of(kind, b, 1 - y, a)
@@ -203,30 +207,36 @@
     keep = pltpu.make_async_copy(own, units.at[mine], own_sem.at[0])
     keep.start()
 
-    fetch.wait()
     count = -(-width // LANE)
     low_ref[:, (count - 1) * LANE :] = jnp.zeros((rows * grads, LANE), BF16)
 
-    def narrow(tile):
+    def narrow(part, tile):
+        if tile == 0:
+            fetch(part).wait()
         left = tile * LANE
         now = min(LANE, width - left)
         column[:, 0:now] = raw[:, left : left + now]
         for g in range(grads):
-            picked = column[pl.ds(g, rows, stride=grads), :].astype(BF16)
-            low_ref[g * rows : (g + 1) * rows, left : left + now] = picked[:, 0:now]
+            picked = column[pl.ds(g, part_rows, stride=grads), :].astype(BF16)
+            at = g * rows + part * part_rows
+            low_ref[at : at + part_rows, left : left + now] = picked[:, 0:now]
+        if tile == count - 1 and part < rows // part_rows - 1:
+            fetch(part + 1).start()
 
     def widen(tile):
         wide_ref[:, tile * LANE : (tile + 1) * LANE] = select(
             lambda t: low_ref[:, t * LANE : (t + 1) * LANE], in_table, in_table_ref, tile
         )
 
-    pieces = [functools.partial(narrow, t) for t in range(count)]
+    pieces = [functools.partial(narrow, part, t) for part in range(rows // part_rows) for t in range(count)]
     pieces += [functools.partial(widen, t) for t in range(wide // LANE)]
     step = functools.partial
     events = [
         step(low_row, 3), step(low_row, 1), step(plane, 1), step(low_near, 0), step(plane, 2), step(plane, 3),
         step(near, 0), step(low_row, 2), step(low_near, 3), step(plane, 4), step(plane, 5), step(low_near, 1),
         step(near, 1), step(low_near, 2), step(plane, 6), step(near, 2), step(plane, 7), step(near, 3),
+        step(low_far, 0), step(low_far, 1), step(near, 4), step(low_far, 2), step(low_far, 3), step(near, 5),
+        step(near, 6), step(near, 7),
     ]
     for at, piece in enumerate(pieces):
         piece()
@@ -264,65 +274,60 @@
     keep_low.wait()
     third = blocks // 3
     beside(0)
-    multiply(0, 0, third)
-    low_far(0)
-    low_far(1)
-    near(4)
-    multiply(0, third, 2 * third)
-    low_far(2)
-    low_far(3)
-    near(5)
-    multiply(0, 2 * third, blocks)
-    near(6)
-    near(7)
     for da in range(X):
         low_across(0, da)
+    for turn in range(3):
+        multiply(0, turn * third, (turn + 1) * third)
+        low_across(3, turn)
+    far(0)
+    low_across(3, 3)
     beside(1)
-    multiply(1, 0, third)
-    far(0)
-    multiply(1, third, 2 * third)
-    far(1)
-    multiply(1, 2 * third, blocks)
-    far(2)
-    for da in range(X):
-        low_across(3, da)
+    for turn in range(3):
+        multiply(1, turn * third, (turn + 1) * third)
+        far(1 + turn)
     beside(3)
-    multiply(3, 0, third)
-    far(3)
-    multiply(3, third, 2 * third)
-    far(4)
-    multiply(3, 2 * third, blocks)
-    far(5)
+    for turn in range(3):
+        multiply(3, turn * third, (turn + 1) * third)
+        far(4 + turn)
     for da in range(X):
         low_across(1, da)
-    far(6)
     far(7)
     beside(2)
+
+    lanes = rows * grads // LANE
+    many = stage.shape[1]
+    batch = many * pad // block
+    rounds = DEVICES // many
 
     def out_copy(n):
         return pltpu.make_async_copy(
             stage.at[n % 2],
-            turned_ref.at[pl.ds(pl.multiple_of(n * block, block), block)],
+            turned_ref.at[pl.ds(n * many, many)],
             stage_sem.at[n % 2],
         )
 
     def last(n, carry):
-        at = pl.ds(pl.multiple_of(n * block, block), block)
+        for k in range(batch):
+            part_n = n * batch + k
+            at = pl.ds(pl.multiple_of(part_n * block, block), block)
+            turned = (total[:, at] + part(2, part_n)).astype(BF16).T.astype(F32)
+            for t in range(lanes):
+                spread[pl.ds(k * block * lanes + t, block, stride=lanes), :] = turned[:, t * LANE : (t + 1) * LANE]
 
         @pl.when(n >= 2)
         def _():
             out_copy(n - 2).wait()
 
-        stage[n % 2] = (total[:, at] + part(2, n)).astype(BF16).T
+        for d in range(many):
+            stage[n % 2, d] = spread[d * pad * lanes : (d * pad + span) * lanes, :].astype(BF16)
         out_copy(n).start()
         return carry
 
-    lax.fori_loop(0, third, last, 0)
+    lax.fori_loop(0, rounds, last, 0)
     for da in range(X):
         low_across(2, da)
-    lax.fori_loop(third, blocks, last, 0)
-    out_copy(blocks - 2).wait()
-    out_copy(blocks - 1).wait()
+    out_copy(rounds - 2).wait()
+    out_copy(rounds - 1).wait()
     low_beside()
     sends = 6 + 4 + 3 * (PLANE - 1) + 3 * PLANE + PLANE
     pltpu.make_async_copy(units.at[pl.ds(0, sends)], units.at[pl.ds(0, sends)], w_send).wait()
@@ -345,11 +350,12 @@
     col_table = wanted(list(range(DEVICES)), span, pad)
     any_space = pl.BlockSpec(memory_space=pl.ANY)
     vmem = pl.BlockSpec(memory_space=pltpu.VMEM)
-    block = 256
+    lanes = rows * grads // LANE
+    many = 16
     return pl.pallas_call(
         functools.partial(rotate_kernel, rows, grads, span, pad, width, in_table, col_table),
         out_shape=(
-            jax.ShapeDtypeStruct((wide, rows * grads), BF16),
+            jax.ShapeDtypeStruct((DEVICES, span * lanes, LANE), BF16),
             jax.ShapeDtypeStruct((DEVICES,) + low_out.shape, BF16),
         ),
         in_specs=[vmem, any_space, any_space, vmem, vmem],
@@ -357,12 +363,13 @@
         scratch_shapes=[
             pltpu.VMEM((DEVICES, pad, wide), BF16),
             pltpu.VMEM((pad, wide), BF16),
-            pltpu.VMEM((rows * grads, width), F32),
-            pltpu.VMEM((rows * grads, LANE), F32),
+            pltpu.VMEM((rows * grads // 2, width), F32),
+            pltpu.VMEM((rows * grads // 2, LANE), F32),
             pltpu.VMEM((rows * grads, up(width, LANE)), BF16),
             pltpu.VMEM((rows * grads, wide), BF16),
             pltpu.VMEM((rows * grads, wide), F32),
-            pltpu.VMEM((2, block, rows * grads), BF16),
+            pltpu.VMEM((many * pad * lanes, LANE), F32),
+            pltpu.VMEM((2, many, span * lanes, LANE), BF16),
             pltpu.SemaphoreType.DMA,
             pltpu.SemaphoreType.DMA((DEVICES,)),
             pltpu.SemaphoreType.DMA,
@@ -383,14 +390,11 @@
     )
 
 
-def finish_kernel(grads, span, pad, group, moved_ref, basis_ref, seed_ref, out_ref, eigen_ref, ready, sem):
+def finish_kernel(grads, span, group, moved_ref, basis_ref, seed_ref, out_ref, eigen_ref, spread):
     rows = LANE // group
-    sources = moved_ref.shape[0]
-    step = pl.program_id(0)
-    tile = basis_ref.shape[1]
-    halves = tile // LANE
-
-    @pl.when(step == 0)
+    sources, depth = moved_ref.shape[:2]
+
+    @pl.when(pl.program_id(0) == 0)
     def _():
         side = group * LANE
         source = lax.broadcasted_iota(jnp.int32, (side, side), 0)
@@ -399,71 +403,32 @@
         chunk = lax.shift_right_logical(source & (LANE - 1), rows.bit_length() - 1)
         outer = lax.shift_right_logical(source, LANE.bit_length() - 1)
         swap = (target == chunk * LANE + outer * rows + inner).astype(F32).astype(BF16)
-        tiles = grads // group
 
         def gather(block, carry):
-            parts = []
-            for tile in range(tiles):
-                parts.append(
-                    jnp.concatenate(
-                        [
-                            moved_ref[block * group + s, :, tile * LANE : (tile + 1) * LANE]
-                            for s in range(group)
-                        ],
-                        axis=1,
-                    )
-                )
-            swapped = jnp.dot(jnp.concatenate(parts, axis=0), swap, preferred_element_type=F32).astype(BF16)
+            parts = [moved_ref[block * group + s] for s in range(group)]
+            swapped = jnp.dot(jnp.concatenate(parts, axis=1), swap, preferred_element_type=F32)
+            for c in range(group):
+                spread[pl.ds(c, depth, stride=group), :] = swapped[:, c * LANE : (c + 1) * LANE]
             at = pl.ds(pl.multiple_of(block * LANE, LANE), LANE)
-            for tile in range(tiles):
-                for c in range(group):
-                    g = tile * group + c
-                    eigen_ref[g * pad : (g + 1) * pad, at] = swapped[
-                        tile * pad : (tile + 1) * pad, c * LANE : (c + 1) * LANE
-                    ]
+            eigen_ref[:, at] = spread[...].astype(BF16)
             return carry
 
         lax.fori_loop(0, sources // group, gather, 0)
 
-    def out_copy(which, half):
-        return pltpu.make_async_copy(
-            ready.at[which % 2, half],
-            out_ref.at[:, pl.ds(pl.multiple_of((which * halves + half) * LANE, LANE), LANE)],
-            sem.at[which % 2, half],
-        )
-
-    @pl.when(step >= 2)
-    def _():
-        for half in range(halves):
-            out_copy(step - 2, half).wait()
-
     value = jnp.exp2(seed_ref[...].astype(F32) * 0.125 - 4.0)
-    denom = value + 0.1
-    for g in range(0, grads, 8):
-        both = jnp.dot(eigen_ref[g * pad : (g + 8) * pad, :], basis_ref[...], preferred_element_type=F32)
-        for d in range(8):
-            result = both[d * pad : d * pad + span, :] / denom
-            for half in range(halves):
-                ready[step % 2, half, pl.ds(g + d, span, stride=grads), :] = result[
-                    :, half * LANE : (half + 1) * LANE
-                ]
-    for half in range(halves):
-        out_copy(step, half).start()
-
-    @pl.when(step == pl.num_programs(0) - 1)
-    def _():
-        for half in range(halves):
-            out_copy(step - 1, half).wait()
-            out_copy(step, half).wait()
+    factor = 1.0 / (value + 0.1)
+    both = jnp.dot(eigen_ref[...], basis_ref[...], preferred_element_type=F32)
+    for c in range(span):
+        out_ref[c * grads : (c + 1) * grads, :] = both[c * grads : (c + 1) * grads, :] * factor[c : c + 1, :]
 
 
 def finish(moved, basis, seeds, grads):
-    span, pad = seeds.shape[0], moved.shape[1]
+    span = seeds.shape[0]
     width = basis.shape[0]
     rows = width // moved.shape[0]
     tile = 256
     return pl.pallas_call(
-        functools.partial(finish_kernel, grads, span, pad, LANE // rows),
+        functools.partial(finish_kernel, grads, span, LANE // rows),
         grid=(width // tile,),
         out_shape=jax.ShapeDtypeStruct((span * grads, width), F32),
         in_specs=[
@@ -471,11 +436,10 @@
             pl.BlockSpec((width, tile), lambda n: (0, n)),
             pl.BlockSpec((span, tile), lambda n: (0, n)),
         ],
-        out_specs=pl.BlockSpec(memory_space=pl.ANY),
+        out_specs=pl.BlockSpec((span * grads, tile), lambda n: (0, n)),
         scratch_shapes=[
-            pltpu.VMEM((pad * grads, width), BF16),
-            pltpu.VMEM((2, tile // LANE, span * grads, LANE), F32),
-            pltpu.SemaphoreType.DMA((2, tile // LANE)),
+            pltpu.VMEM((span * grads, width), BF16),
+            pltpu.VMEM((span * grads, LANE), F32),
         ],
         compiler_params=pltpu.CompilerParams(vmem_limit_bytes=56 << 20),
     )(moved, basis, seeds)
@@ -485,7 +449,6 @@
     rows, grads, width = gradients.shape
     pad = up(in_basis.shape[0], 16)
     rotated, full_out = rotate(gradients, in_basis, out_basis, pad)
-    rotated = rotated.reshape(DEVICES, pad, rows * grads)
     moved = lax.all_to_all(rotated, "rows", split_axis=0, concat_axis=0, tiled=True)
     full_out = full_out.reshape(-1, out_basis.shape[1])
     return finish(moved, full_out, eigen_seeds, grads).T

time: 208 us -> 202 us (0.971)
  blocking collectives: 82.8 us -> 78.2 us
    pallas_call x1, Pallas kernels: 32.5 us -> 25.1 us  [finish(): pl.pallas_call(functools.partial(finish_kernel, grads, span, LANE // rows...]
    pallas_call x1, Pallas kernels: 92.6 us -> 98.2 us  [rotate(): pl.pallas_call(functools.partial(rotate_kernel, rows, grads, span, pad, w...]
    all_to_all x1, blocking collectives: 82.8 us -> 78.2 us  [local(): lax.all_to_all(rotated, 'rows', split_axis=0, concat_axis=0, tiled=True)]
where the time goes in v4:
time: 202 us
  Pallas kernels  123 us (61%)
  blocking collectives  78.2 us (39%)
    pallas_call x1, Pallas kernels, rotate(): pl.pallas_call(functools.partial(rotate_kernel, rows, grads, span, pad, w...  98.2 us
    all_to_all x1, blocking collectives, local(): lax.all_to_all(rotated, 'rows', split_axis=0, concat_axis=0, tiled=True)  78.2 us
    pallas_call x1, Pallas kernels, finish(): pl.pallas_call(functools.partial(finish_kernel, grads, span, LANE // rows...  25.1 us

profile of v4, /device:TPU:1, one launch (start us, length us, event | category | flops | bytes accessed | tf_op | source)
XLA Modules:
  0.0 201.5 jit_solution(9327435870321346151)
XLA Ops:
  0.0 98.2 %shard_map.64 = (bf16[64,360,128]{2,1,0:T(8,128)(2,1)}, bf16[64,32,2048]{2,1,0:T(8,128)(2,1)}) custom-call(bf16[45,2880]{1,0:T(8,128)(2,1)} %shard_ref.1, bf16[32,2048]{1,0:T(8,128)(2,1)} %low_out_ref.1, f32[1024,2880]{1,0:T(8,128)} %bitcast.3, s32[24,1,128]{2,1,0:T(1,128)} %constant.4.clone.in_table_ref, s32[24,1,128]{2,1,0:T(1,128)} %constant.5.clone.col_table_ref), custom_call_target="tpu_custom_call" | custom-call | tf_op jit(solution)/shard_map/pallas_call | solution.py:355
  98.2 78.2 %all_to_all.5.moved_ref = bf16[64,360,128]{2,1,0:T(8,128)(2,1)} all-to-all(bf16[64,360,128]{2,1,0:T(8,128)(2,1)} %get-tuple-element.7), channel_id=1, replica_groups=mesh['rows'=64,'layer'=2] {'rows'}, dimensions={0} | all-to-all | bytes 11796480 | tf_op jit(solution)/shard_map/all_to_all | solution.py:452
  176.4 25.1 %shard_map.65 = f32[1440,2048]{1,0:T(8,128)} custom-call(bf16[64,360,128]{2,1,0:T(8,128)(2,1)} %all_to_all.5.moved_ref, bf16[2048,2048]{1,0:T(8,128)(2,1)} %bitcast.4, s32[45,2048]{1,0:T(8,128)} %seed_ref.1), custom_call_target="tpu_custom_call" | custom-call | tf_op jit(solution)/shard_map/pallas_call | solution.py:430

commit v5 on v4

--- a/solution.py
+++ b/solution.py
@@ -233,10 +233,8 @@
     step = functools.partial
     events = [
         step(low_row, 3), step(low_row, 1), step(plane, 1), step(low_near, 0), step(plane, 2), step(plane, 3),
-        step(near, 0), step(low_row, 2), step(low_near, 3), step(plane, 4), step(plane, 5), step(low_near, 1),
-        step(near, 1), step(low_near, 2), step(plane, 6), step(near, 2), step(plane, 7), step(near, 3),
-        step(low_far, 0), step(low_far, 1), step(near, 4), step(low_far, 2), step(low_far, 3), step(near, 5),
-        step(near, 6), step(near, 7),
+        step(low_row, 2), step(low_near, 3), step(plane, 4), step(plane, 5), step(low_near, 1), step(plane, 6),
+        step(plane, 7), step(low_near, 2),
     ]
     for at, piece in enumerate(pieces):
         piece()
@@ -272,25 +270,31 @@
 
     keep.wait()
     keep_low.wait()
-    third = blocks // 3
+    near(0)
+    near(1)
+    low_far(0)
+    near(2)
+    low_far(1)
     beside(0)
-    for da in range(X):
-        low_across(0, da)
-    for turn in range(3):
-        multiply(0, turn * third, (turn + 1) * third)
+    for turn in range(6):
+        multiply(0, turn * blocks // 6, (turn + 1) * blocks // 6)
+        if turn < 5:
+            near(3 + turn)
+        if turn < 2:
+            low_far(2 + turn)
+        elif turn < 6:
+            low_across(0, turn - 2)
+    beside(1)
+    for turn in range(4):
+        multiply(1, turn * blocks // 4, (turn + 1) * blocks // 4)
+        far(turn)
         low_across(3, turn)
-    far(0)
-    low_across(3, 3)
-    beside(1)
-    for turn in range(3):
-        multiply(1, turn * third, (turn + 1) * third)
-        far(1 + turn)
     beside(3)
-    for turn in range(3):
-        multiply(3, turn * third, (turn + 1) * third)
-        far(4 + turn)
-    for da in range(X):
-        low_across(1, da)
+    for turn in range(4):
+        multiply(3, turn * blocks // 4, (turn + 1) * blocks // 4)
+        low_across(1, turn)
+        if turn < 3:
+            far(4 + turn)
     far(7)
     beside(2)
 

time: 202 us -> 194 us (0.960)
  Pallas kernels: 123 us -> 113 us
    pallas_call x1, Pallas kernels: 98.2 us -> 87.9 us  [rotate(): pl.pallas_call(functools.partial(rotate_kernel, rows, grads, span, pad, w...]
where the time goes in v5:
time: 194 us; the launch traced here: 193 us
  Pallas kernels  113 us (58%)
  blocking collectives  80.1 us (41%)
    pallas_call x1, Pallas kernels, rotate(): pl.pallas_call(functools.partial(rotate_kernel, rows, grads, span, pad, w...  87.9 us
    all_to_all x1, blocking collectives, local(): lax.all_to_all(rotated, 'rows', split_axis=0, concat_axis=0, tiled=True)  80.1 us
    pallas_call x1, Pallas kernels, finish(): pl.pallas_call(functools.partial(finish_kernel, grads, span, LANE // rows...  25.1 us

profile of v5, /device:TPU:1, one launch (start us, length us, event | category | flops | bytes accessed | tf_op | source)
XLA Modules:
  0.0 193.1 jit_solution(12139376316454606219)
XLA Ops:
  0.0 87.9 %shard_map.64 = (bf16[64,360,128]{2,1,0:T(8,128)(2,1)}, bf16[64,32,2048]{2,1,0:T(8,128)(2,1)}) custom-call(bf16[45,2880]{1,0:T(8,128)(2,1)} %shard_ref.1, bf16[32,2048]{1,0:T(8,128)(2,1)} %low_out_ref.1, f32[1024,2880]{1,0:T(8,128)} %bitcast.3, s32[24,1,128]{2,1,0:T(1,128)} %constant.4.clone.in_table_ref, s32[24,1,128]{2,1,0:T(1,128)} %constant.5.clone.col_table_ref), custom_call_target="tpu_custom_call" | custom-call | tf_op jit(solution)/shard_map/pallas_call | solution.py:359
  87.9 80.1 %all_to_all.5.moved_ref = bf16[64,360,128]{2,1,0:T(8,128)(2,1)} all-to-all(bf16[64,360,128]{2,1,0:T(8,128)(2,1)} %get-tuple-element.7), channel_id=1, replica_groups=mesh['rows'=64,'layer'=2] {'rows'}, dimensions={0} | all-to-all | bytes 11796480 | tf_op jit(solution)/shard_map/all_to_all | solution.py:456
  168.0 25.1 %shard_map.65 = f32[1440,2048]{1,0:T(8,128)} custom-call(bf16[64,360,128]{2,1,0:T(8,128)(2,1)} %all_to_all.5.moved_ref, bf16[2048,2048]{1,0:T(8,128)(2,1)} %bitcast.4, s32[45,2048]{1,0:T(8,128)} %seed_ref.1), custom_call_target="tpu_custom_call" | custom-call | tf_op jit(solution)/shard_map/pallas_call | solution.py:434
